TPU v7x, 32 devices: a whole 2x2x4 slice. The times are simulated.
32 devices in a mesh: site: 4 (over y, x), sector: 8 (over z, core).
Axes of the slice: x: 2, y: 2, z: 4, core: 2. Of those that a mesh axis runs over, the one named last changes fastest.
Arguments:
- boundary: bfloat16 [4, 2048, 32, 256], P('site', 'sector'), may hold values from -0.375 to 0.375
- peps_row: bfloat16 [4, 32, 8], P('site'), may hold values from -1 to 1
- sketch: bfloat16 [4, 2048, 8, 256], P('site', 'sector'), may hold values from -0.125 to 0.125
- charges: int32 [4, 8], P('site'), may hold values from -1 to 1
- left_edge: bfloat16 [512, 2048], P(None, 'sector'), may hold values from -6 to 6
Outputs:
- environments: float32 [4, 512, 2048], P('site', None, 'sector')
Inputs may be any that keep to these rules, and one draw needn't show every extreme that they name: `charges`: each entry is a charge change of -1, 0 or +1.
All inputs are finite; a program needn't handle non-finite values.
Results may differ from a plain program's by a relative error of at most 0.0003.
Values sent between devices are 32-bit elements; how exact they have to be, the bound alone decides.
A program may use at most 64 MiB of HBM per device.

v0:
```python
import jax
import jax.numpy as jnp
from jax import lax
from jax.sharding import PartitionSpec as P


def with_halo(block, sides, width):
    for axis, dim in sides:
        count = lax.axis_size(axis)
        forward = [(i, i + 1) for i in range(count - 1)]
        backward = [(target, source) for source, target in forward]
        low = lax.ppermute(
            lax.slice_in_dim(block, block.shape[dim] - width, None, axis=dim), axis, forward
        )
        high = lax.ppermute(lax.slice_in_dim(block, 0, width, axis=dim), axis, backward)
        block = jnp.concatenate([low, block, high], axis=dim)
    return block


def local(boundary, peps_row, sketch, charges, left_edge):
    total_rows = left_edge.shape[0]
    absorbed = jnp.einsum("jwpv,jpl->jwlv", boundary, peps_row, preferred_element_type=jnp.float32)
    sketch_wide = sketch.astype(jnp.float32)
    onehot = (charges[:, :, None] == jnp.arange(-1, 2, dtype=jnp.int32)[None, None, :]).astype(
        jnp.float32
    )
    site_devices = lax.axis_size("site")
    position = lax.axis_index("site")
    own_maps = jnp.einsum(
        "jwlv,jvlu,jls->jswu", absorbed, sketch_wide, onehot, precision=lax.Precision.HIGHEST
    )
    all_maps = lax.all_gather(own_maps, "site", axis=0, tiled=True)
    share_rows = total_rows // site_devices
    start_state = lax.dynamic_slice_in_dim(left_edge, position * share_rows, share_rows, 0).astype(
        jnp.float32
    )

    def row_site(state_rows, site_map):
        parts = jnp.einsum("rw,swu->sru", state_rows, site_map, precision=lax.Precision.HIGHEST)
        outflow = jnp.stack([parts[0], parts[2]], axis=0)
        padded = with_halo(outflow, (("sector", 0),), 1)
        updated = parts[1] + padded[0] + padded[3]
        return (updated, updated)

    final_rows, stacked = lax.scan(row_site, start_state, all_maps)
    return lax.all_to_all(stacked, "site", split_axis=0, concat_axis=1, tiled=True)


def solution(mesh):
    in_specs = (
        P("site", "sector", None, None),
        P("site", None, None),
        P("site", "sector", None, None),
        P("site", None),
        P(None, "sector"),
    )
    out_specs = P("site", None, "sector")
    return jax.shard_map(local, mesh=mesh, in_specs=in_specs, out_specs=out_specs, check_vma=False)
```

profile of v0, /device:TPU:8, one launch (start us, length us, event | category | flops | bytes accessed | tf_op | source)
XLA Modules:
  0.0 126.1 jit_solution(7024198187606349648)
XLA Ops:
  6.5 2.9 %fusion.12 = f32[256,8,256]{2,1,0:T(8,128)S(1)} fusion(bf16[1,256,32,256]{3,2,1,0:T(8,128)(2,1)} %param.7, bf16[1,32,8]{1,2,0:T(8,128)(2,1)} %param.8), kind=kOutput, calls=%fused_computation.15 | convolution fusion | flops 33554432 | bytes 6291968 | tf_op jit(solution)/shard_map/jwpv,jpl->jwlv/dot_general | solution.py:22
  9.5 3.1 %fusion.10 = f32[8,256,256]{2,1,0:T(8,128)} fusion(f32[256,8,256]{2,1,0:T(8,128)S(1)} %fusion.12, bf16[256,8,256]{2,1,0:T(8,128)(2,1)S(1)} %bitcast.47), kind=kOutput, calls=%fused_computation.13 | convolution fusion | flops 1610612736 | bytes 5242880 | tf_op jit(solution)/shard_map/jwlv,jvlu,jls->jswu/dot_general | solution.py:29
  12.6 2.2 %copy.18 = f32[8,256,256]{1,0,2:T(8,128)S(1)} copy(f32[8,256,256]{2,1,0:T(8,128)} %fusion.10) | data formatting | bytes 4194304 | tf_op jit(solution)/shard_map/jwlv,jvlu,jls->jswu/dot_general | solution.py:29
  14.8 2.1 %fusion.15 = f32[1,3,256,256]{2,1,3,0:T(4,128)} fusion(f32[8,256,256]{1,0,2:T(8,128)S(1)} %copy.18, s32[8]{0:T(128)S(1)} %bitcast.48, s32[3]{0:T(128)S(1)} %iota_add_fusion), kind=kOutput, calls=%fused_computation.16 | convolution fusion | flops 18874392 | bytes 2883628 | tf_op jit(solution)/shard_map/jwlv,jvlu,jls->jswu/dot_general | solution.py:29
  16.9 2.4 %copy.12 = f32[1,3,256,256]{3,2,1,0:T(8,128)} copy(f32[1,3,256,256]{2,1,3,0:T(4,128)} %fusion.15) | data formatting | bytes 1572864 | tf_op jit(solution)/shard_map/jwlv,jvlu,jls->jswu/transpose | solution.py:29
  20.3 44.2 %all-gather.2.cloned.1.call-done = f32[4,3,256,256]{3,2,1,0:T(8,128)} async-done(((f32[1,3,256,256]{3,2,1,0:T(8,128)}), f32[4,3,256,256]{3,2,1,0:T(8,128)}) %all-gather.2.cloned.1.call-update) | async-done | bytes 3145744 | tf_op jit(solution)/shard_map/all_gather | solution.py:32
  64.5 43.3 %while.12 = (s32[]{:T(128)}, f32[128,256]{0,1:T(8,128)S(1)}, f32[4,128,256]{1,2,0:T(8,128)S(1)}, f32[4,3,256,256]{3,2,1,0:T(8,128)}, s32[]{:T(128)}) while((s32[]{:T(128)}, f32[128,256]{0,1:T(8,128)S(1)}, f32[4,128,256]{1,2,0:T(8,128)S(1)}, f32[4,3,256,256]{3,2,1,0:T(8,128)}, s32[]{:T(128)}) %tuple.26), condition=%wide.region_1.2_spmd, body=%wide.region_0.1_spmd.sunk | while | flops 302055424 | bytes 3539101 | solution.py:45
  64.5 2.5 %convolution_bitcast_fusion.2 = f32[3,128,256]{1,2,0:T(8,128)S(1)} fusion(f32[4,3,256,256]{3,2,1,0:T(8,128)} %get-tuple-element.94, s32[]{:T(128)S(6)} %copy.30, f32[128,256]{0,1:T(8,128)S(1)} %get-tuple-element.87), kind=kOutput, calls=%fused_computation.clone.1 | convolution fusion | flops 301989888 | bytes 1310724 | tf_op jit(solution)/shard_map/while/body/eval_jaxpr/rw,swu->sru/dot_general | solution.py:39
  67.0 1.9 %collective-permute-start = (f32[1,128,256]{1,2,0:T(8,128)S(1)}, f32[1,128,256]{1,2,0:T(8,128)S(1)}, u32[]{:S(2)}, u32[]{:S(2)}) collective-permute-start(f32[1,128,256]{1,2,0:T(8,128)S(1)} %get-tuple-element.77), channel_id=1, source_target_pairs={{1,0},{2,1},{3,2},{4,3},{5,4},{6,5},{7,6},{9,8},{10,9},{11,10},{12... | collective-permute-start | bytes 393224 | tf_op jit(solution)/shard_map/while/body/eval_jaxpr/ppermute | solution.py:15
  69.0 2.4 %collective-permute-start.1 = (f32[1,128,256]{1,2,0:T(8,128)S(1)}, f32[1,128,256]{1,2,0:T(8,128)S(1)}, u32[]{:S(2)}, u32[]{:S(2)}) collective-permute-start(f32[1,128,256]{1,2,0:T(8,128)S(1)} %get-tuple-element.78), channel_id=1, source_target_pairs={{0,1},{1,2},{2,3},{3,4},{4,5},{5,6},{6,7},{8,9},{9,10},{10,11},{11... | collective-permute-start | bytes 393224 | tf_op jit(solution)/shard_map/while/body/eval_jaxpr/ppermute | solution.py:12
  71.5 3.8 %collective-permute-done.1 = f32[1,128,256]{1,2,0:T(8,128)S(1)} collective-permute-done((f32[1,128,256]{1,2,0:T(8,128)S(1)}, f32[1,128,256]{1,2,0:T(8,128)S(1)}, u32[]{:S(2)}, u32[]{:S(2)}) %collective-permute-start.1) | collective-permute-done | bytes 131104 | tf_op jit(solution)/shard_map/while/body/eval_jaxpr/ppermute | solution.py:12
  75.3 2.5 %convolution_bitcast_fusion.2 = f32[3,128,256]{1,2,0:T(8,128)S(1)} fusion(f32[4,3,256,256]{3,2,1,0:T(8,128)} %get-tuple-element.94, s32[]{:T(128)S(6)} %copy.30, f32[128,256]{0,1:T(8,128)S(1)} %get-tuple-element.87), kind=kOutput, calls=%fused_computation.clone.1 | convolution fusion | flops 301989888 | bytes 1310724 | tf_op jit(solution)/shard_map/while/body/eval_jaxpr/rw,swu->sru/dot_general | solution.py:39
  77.9 1.9 %collective-permute-start = (f32[1,128,256]{1,2,0:T(8,128)S(1)}, f32[1,128,256]{1,2,0:T(8,128)S(1)}, u32[]{:S(2)}, u32[]{:S(2)}) collective-permute-start(f32[1,128,256]{1,2,0:T(8,128)S(1)} %get-tuple-element.77), channel_id=1, source_target_pairs={{1,0},{2,1},{3,2},{4,3},{5,4},{6,5},{7,6},{9,8},{10,9},{11,10},{12... | collective-permute-start | bytes 393224 | tf_op jit(solution)/shard_map/while/body/eval_jaxpr/ppermute | solution.py:15
  79.8 2.4 %collective-permute-start.1 = (f32[1,128,256]{1,2,0:T(8,128)S(1)}, f32[1,128,256]{1,2,0:T(8,128)S(1)}, u32[]{:S(2)}, u32[]{:S(2)}) collective-permute-start(f32[1,128,256]{1,2,0:T(8,128)S(1)} %get-tuple-element.78), channel_id=1, source_target_pairs={{0,1},{1,2},{2,3},{3,4},{4,5},{5,6},{6,7},{8,9},{9,10},{10,11},{11... | collective-permute-start | bytes 393224 | tf_op jit(solution)/shard_map/while/body/eval_jaxpr/ppermute | solution.py:12
  82.3 3.8 %collective-permute-done.1 = f32[1,128,256]{1,2,0:T(8,128)S(1)} collective-permute-done((f32[1,128,256]{1,2,0:T(8,128)S(1)}, f32[1,128,256]{1,2,0:T(8,128)S(1)}, u32[]{:S(2)}, u32[]{:S(2)}) %collective-permute-start.1) | collective-permute-done | bytes 131104 | tf_op jit(solution)/shard_map/while/body/eval_jaxpr/ppermute | solution.py:12
  86.1 2.5 %convolution_bitcast_fusion.2 = f32[3,128,256]{1,2,0:T(8,128)S(1)} fusion(f32[4,3,256,256]{3,2,1,0:T(8,128)} %get-tuple-element.94, s32[]{:T(128)S(6)} %copy.30, f32[128,256]{0,1:T(8,128)S(1)} %get-tuple-element.87), kind=kOutput, calls=%fused_computation.clone.1 | convolution fusion | flops 301989888 | bytes 1310724 | tf_op jit(solution)/shard_map/while/body/eval_jaxpr/rw,swu->sru/dot_general | solution.py:39
  88.7 1.9 %collective-permute-start = (f32[1,128,256]{1,2,0:T(8,128)S(1)}, f32[1,128,256]{1,2,0:T(8,128)S(1)}, u32[]{:S(2)}, u32[]{:S(2)}) collective-permute-start(f32[1,128,256]{1,2,0:T(8,128)S(1)} %get-tuple-element.77), channel_id=1, source_target_pairs={{1,0},{2,1},{3,2},{4,3},{5,4},{6,5},{7,6},{9,8},{10,9},{11,10},{12... | collective-permute-start | bytes 393224 | tf_op jit(solution)/shard_map/while/body/eval_jaxpr/ppermute | solution.py:15
  90.6 2.4 %collective-permute-start.1 = (f32[1,128,256]{1,2,0:T(8,128)S(1)}, f32[1,128,256]{1,2,0:T(8,128)S(1)}, u32[]{:S(2)}, u32[]{:S(2)}) collective-permute-start(f32[1,128,256]{1,2,0:T(8,128)S(1)} %get-tuple-element.78), channel_id=1, source_target_pairs={{0,1},{1,2},{2,3},{3,4},{4,5},{5,6},{6,7},{8,9},{9,10},{10,11},{11... | collective-permute-start | bytes 393224 | tf_op jit(solution)/shard_map/while/body/eval_jaxpr/ppermute | solution.py:12
  93.1 3.8 %collective-permute-done.1 = f32[1,128,256]{1,2,0:T(8,128)S(1)} collective-permute-done((f32[1,128,256]{1,2,0:T(8,128)S(1)}, f32[1,128,256]{1,2,0:T(8,128)S(1)}, u32[]{:S(2)}, u32[]{:S(2)}) %collective-permute-start.1) | collective-permute-done | bytes 131104 | tf_op jit(solution)/shard_map/while/body/eval_jaxpr/ppermute | solution.py:12
  96.9 2.5 %convolution_bitcast_fusion.2 = f32[3,128,256]{1,2,0:T(8,128)S(1)} fusion(f32[4,3,256,256]{3,2,1,0:T(8,128)} %get-tuple-element.94, s32[]{:T(128)S(6)} %copy.30, f32[128,256]{0,1:T(8,128)S(1)} %get-tuple-element.87), kind=kOutput, calls=%fused_computation.clone.1 | convolution fusion | flops 301989888 | bytes 1310724 | tf_op jit(solution)/shard_map/while/body/eval_jaxpr/rw,swu->sru/dot_general | solution.py:39
  99.5 1.9 %collective-permute-start = (f32[1,128,256]{1,2,0:T(8,128)S(1)}, f32[1,128,256]{1,2,0:T(8,128)S(1)}, u32[]{:S(2)}, u32[]{:S(2)}) collective-permute-start(f32[1,128,256]{1,2,0:T(8,128)S(1)} %get-tuple-element.77), channel_id=1, source_target_pairs={{1,0},{2,1},{3,2},{4,3},{5,4},{6,5},{7,6},{9,8},{10,9},{11,10},{12... | collective-permute-start | bytes 393224 | tf_op jit(solution)/shard_map/while/body/eval_jaxpr/ppermute | solution.py:15
  101.4 2.4 %collective-permute-start.1 = (f32[1,128,256]{1,2,0:T(8,128)S(1)}, f32[1,128,256]{1,2,0:T(8,128)S(1)}, u32[]{:S(2)}, u32[]{:S(2)}) collective-permute-start(f32[1,128,256]{1,2,0:T(8,128)S(1)} %get-tuple-element.78), channel_id=1, source_target_pairs={{0,1},{1,2},{2,3},{3,4},{4,5},{5,6},{6,7},{8,9},{9,10},{10,11},{11... | collective-permute-start | bytes 393224 | tf_op jit(solution)/shard_map/while/body/eval_jaxpr/ppermute | solution.py:12
  103.9 3.8 %collective-permute-done.1 = f32[1,128,256]{1,2,0:T(8,128)S(1)} collective-permute-done((f32[1,128,256]{1,2,0:T(8,128)S(1)}, f32[1,128,256]{1,2,0:T(8,128)S(1)}, u32[]{:S(2)}, u32[]{:S(2)}) %collective-permute-start.1) | collective-permute-done | bytes 131104 | tf_op jit(solution)/shard_map/while/body/eval_jaxpr/ppermute | solution.py:12
  107.8 10.5 %all_to_all.12 = f32[4,128,256]{1,2,0:T(8,128)S(1)} all-to-all(f32[4,128,256]{1,2,0:T(8,128)S(1)} %get-tuple-element.27), channel_id=1, replica_groups=mesh['site'=4,'sector'=8] {'site'}, dimensions={0} | all-to-all | bytes 1048576 | tf_op jit(solution)/shard_map/all_to_all | solution.py:46
  (24 shorter events, 2.5 us)
Async XLA Ops:
  6.5 3.0 %copy-start = (bf16[1,256,8,256]{3,2,1,0:T(8,128)(2,1)S(1)}, bf16[1,256,8,256]{3,2,1,0:T(8,128)(2,1)}, u32[]{:S(2)}) copy-start(bf16[1,256,8,256]{3,2,1,0:T(8,128)(2,1)} %param.9) | copy-start | bytes 3145732
  6.5 57.9 %all-gather.2.cloned.1.call-start = ((), (), s32[]{:S(2)}) async-start(), calls=%async_computation.1 | async-start | bytes 3932160 | tf_op jit(solution)/shard_map/all_gather | solution.py:32
  12.6 2.2 %copy-start.1 = (s32[1,8]{1,0:T(1,128)S(1)}, s32[1,8]{1,0:T(1,128)}, u32[]{:S(2)}) copy-start(s32[1,8]{1,0:T(1,128)} %param.10) | copy-start | bytes 100
  67.0 4.4 %collective-permute-start = (f32[1,128,256]{1,2,0:T(8,128)S(1)}, f32[1,128,256]{1,2,0:T(8,128)S(1)}, u32[]{:S(2)}, u32[]{:S(2)}) collective-permute-start(f32[1,128,256]{1,2,0:T(8,128)S(1)} %get-tuple-element.77), channel_id=1, source_target_pairs={{1,0},{2,1},{3,2},{4,3},{5,4},{6,5},{7,6},{9,8},{10,9},{11,10},{12... | collective-permute-start | bytes 393224 | tf_op jit(solution)/shard_map/while/body/eval_jaxpr/ppermute | solution.py:15
  69.0 6.3 %collective-permute-start.1 = (f32[1,128,256]{1,2,0:T(8,128)S(1)}, f32[1,128,256]{1,2,0:T(8,128)S(1)}, u32[]{:S(2)}, u32[]{:S(2)}) collective-permute-start(f32[1,128,256]{1,2,0:T(8,128)S(1)} %get-tuple-element.78), channel_id=1, source_target_pairs={{0,1},{1,2},{2,3},{3,4},{4,5},{5,6},{6,7},{8,9},{9,10},{10,11},{11... | collective-permute-start | bytes 393224 | tf_op jit(solution)/shard_map/while/body/eval_jaxpr/ppermute | solution.py:12
  77.9 4.4 %collective-permute-start = (f32[1,128,256]{1,2,0:T(8,128)S(1)}, f32[1,128,256]{1,2,0:T(8,128)S(1)}, u32[]{:S(2)}, u32[]{:S(2)}) collective-permute-start(f32[1,128,256]{1,2,0:T(8,128)S(1)} %get-tuple-element.77), channel_id=1, source_target_pairs={{1,0},{2,1},{3,2},{4,3},{5,4},{6,5},{7,6},{9,8},{10,9},{11,10},{12... | collective-permute-start | bytes 393224 | tf_op jit(solution)/shard_map/while/body/eval_jaxpr/ppermute | solution.py:15
  79.8 6.3 %collective-permute-start.1 = (f32[1,128,256]{1,2,0:T(8,128)S(1)}, f32[1,128,256]{1,2,0:T(8,128)S(1)}, u32[]{:S(2)}, u32[]{:S(2)}) collective-permute-start(f32[1,128,256]{1,2,0:T(8,128)S(1)} %get-tuple-element.78), channel_id=1, source_target_pairs={{0,1},{1,2},{2,3},{3,4},{4,5},{5,6},{6,7},{8,9},{9,10},{10,11},{11... | collective-permute-start | bytes 393224 | tf_op jit(solution)/shard_map/while/body/eval_jaxpr/ppermute | solution.py:12
  88.7 4.4 %collective-permute-start = (f32[1,128,256]{1,2,0:T(8,128)S(1)}, f32[1,128,256]{1,2,0:T(8,128)S(1)}, u32[]{:S(2)}, u32[]{:S(2)}) collective-permute-start(f32[1,128,256]{1,2,0:T(8,128)S(1)} %get-tuple-element.77), channel_id=1, source_target_pairs={{1,0},{2,1},{3,2},{4,3},{5,4},{6,5},{7,6},{9,8},{10,9},{11,10},{12... | collective-permute-start | bytes 393224 | tf_op jit(solution)/shard_map/while/body/eval_jaxpr/ppermute | solution.py:15
  90.6 6.3 %collective-permute-start.1 = (f32[1,128,256]{1,2,0:T(8,128)S(1)}, f32[1,128,256]{1,2,0:T(8,128)S(1)}, u32[]{:S(2)}, u32[]{:S(2)}) collective-permute-start(f32[1,128,256]{1,2,0:T(8,128)S(1)} %get-tuple-element.78), channel_id=1, source_target_pairs={{0,1},{1,2},{2,3},{3,4},{4,5},{5,6},{6,7},{8,9},{9,10},{10,11},{11... | collective-permute-start | bytes 393224 | tf_op jit(solution)/shard_map/while/body/eval_jaxpr/ppermute | solution.py:12
  99.5 4.4 %collective-permute-start = (f32[1,128,256]{1,2,0:T(8,128)S(1)}, f32[1,128,256]{1,2,0:T(8,128)S(1)}, u32[]{:S(2)}, u32[]{:S(2)}) collective-permute-start(f32[1,128,256]{1,2,0:T(8,128)S(1)} %get-tuple-element.77), channel_id=1, source_target_pairs={{1,0},{2,1},{3,2},{4,3},{5,4},{6,5},{7,6},{9,8},{10,9},{11,10},{12... | collective-permute-start | bytes 393224 | tf_op jit(solution)/shard_map/while/body/eval_jaxpr/ppermute | solution.py:15
  101.4 6.3 %collective-permute-start.1 = (f32[1,128,256]{1,2,0:T(8,128)S(1)}, f32[1,128,256]{1,2,0:T(8,128)S(1)}, u32[]{:S(2)}, u32[]{:S(2)}) collective-permute-start(f32[1,128,256]{1,2,0:T(8,128)S(1)} %get-tuple-element.78), channel_id=1, source_target_pairs={{0,1},{1,2},{2,3},{3,4},{4,5},{5,6},{6,7},{8,9},{9,10},{10,11},{11... | collective-permute-start | bytes 393224 | tf_op jit(solution)/shard_map/while/body/eval_jaxpr/ppermute | solution.py:12
Sparse Core Ops, SparseCore 0:
  19.4 44.9 all-gather.1
where the time goes:
time: 127 us; the launch traced here: 126 us
  waiting for transfers between devices  59.7 us (47%)
  matrix products  18.2 us (14%)
  starting transfers between devices  17.3 us (14%)
  between operations  13.5 us (11%)
  blocking collectives  10.5 us (8%)
  local copies, waits for them, and re-layouts  6.64 us (5%)
    all_gather x1, waiting for transfers between devices, local(): all_maps = lax.all_gather(own_maps, 'site', axis=0, tiled=True)  44.2 us
    ppermute x4, waiting for transfers between devices, with_halo(): lax.ppermute(lax.slice_in_dim(block, block.shape[dim] - width, None, axis...  15.1 us
    all_to_all x1, blocking collectives, local(): lax.all_to_all(stacked, 'site', split_axis=0, concat_axis=1, tiled=True)  10.5 us
    dot_general x4, matrix products, row_site(): jnp.einsum('rw,swu->sru', state_rows, site_map, precision=lax.Precision.H...  10.1 us
    ppermute x4, starting transfers between devices, with_halo(): lax.ppermute(lax.slice_in_dim(block, block.shape[dim] - width, None, axis...  9.63 us
    ppermute x4, starting transfers between devices, with_halo(): lax.ppermute(lax.slice_in_dim(block, 0, width, axis=dim), axis, backward)  7.68 us
    dot_general x2, matrix products, local(): jnp.einsum('jwlv,jvlu,jls->jswu', absorbed, sketch_wide, onehot, precisio...  5.17 us
    dot_general x1, matrix products, local(): jnp.einsum('jwpv,jpl->jwlv', boundary, peps_row, preferred_element_type=j...  2.94 us
  transfers between devices with their start and end apart: 9, of which 9 were waited for; matrix products, arithmetic and copies ran while one was open for 1% of the time, Pallas kernels for 0%

commit v1 on v0

v1 whole, which is shorter than its diff:
```python
import functools

import jax
import jax.numpy as jnp
from jax import lax
from jax.experimental import pallas as pl
from jax.experimental.pallas import tpu as pltpu
from jax.sharding import PartitionSpec as P

MESH = pl.DeviceIdType.MESH
CHUNK_ROWS = 64
LAG = 1
MAP_ROWS = 64


def dot(a, b):
    return jnp.dot(a, b, preferred_element_type=jnp.float32)


def split(x):
    high = x.astype(jnp.bfloat16)
    low = (x - high.astype(jnp.float32)).astype(jnp.bfloat16)
    return high, low


def kernel(
    sites,
    sectors,
    width,
    phys,
    depth,
    boundary_ref,
    peps_ref,
    sketch_ref,
    charges_ref,
    left_ref,
    out_ref,
    boundary,
    sketch,
    absorbed,
    sorted_sketch,
    map_high,
    map_low,
    state,
    from_below,
    from_above,
    upward,
    downward,
    boundary_sem,
    sketch_sem,
    state_send,
    state_recv,
    up_send,
    up_recv,
    down_send,
    down_recv,
):
    site = lax.axis_index("site")
    sector = lax.axis_index("sector")
    rows = left_ref.shape[0]
    chunks = rows // CHUNK_ROWS
    steps = width // MAP_ROWS
    f32, bf16 = jnp.float32, jnp.bfloat16

    sketch_copy = pltpu.make_async_copy(sketch_ref, sketch, sketch_sem)
    sketch_copy.start()
    slab = MAP_ROWS * phys
    slabs = []
    for i in range(steps):
        part = pl.ds(i * slab, slab)
        copy = pltpu.make_async_copy(boundary_ref.at[part], boundary.at[part], boundary_sem.at[i])
        copy.start()
        slabs.append(copy)

    barrier = pltpu.get_barrier_semaphore()
    has_prev, has_next = site > 0, site < sites - 1
    has_below, has_above = sector > 0, sector < sectors - 1

    def greet(condition, target):
        @pl.when(condition)
        def _():
            pl.semaphore_signal(barrier, inc=1, device_id=target, device_id_type=MESH)

    prev_id, next_id = (site - 1, sector), (site + 1, sector)
    below_id, above_id = (site, sector - 1), (site, sector + 1)
    greet(has_prev, prev_id)
    greet(has_next, next_id)
    greet(has_below, below_id)
    greet(has_above, above_id)

    @pl.when(site == 0)
    def _():
        state[...] = left_ref[...].astype(f32)

    group = width // phys
    size = group * depth
    iota = lambda shape, axis: lax.broadcasted_iota(jnp.int32, shape, axis)
    pick = (iota((size, depth), 0) // group == iota((size, depth), 1)).astype(f32).astype(bf16)
    tile = (iota((phys, width), 1) % phys == iota((phys, width), 0)).astype(f32).astype(bf16)
    by_row = dot(pick, peps_ref[...]).astype(bf16)
    same = iota((size, width), 0) % group == iota((size, width), 1) // phys
    spread = jnp.where(same, dot(by_row, tile), 0.0).astype(bf16)

    run = width // depth
    order = (
        iota((width, width), 1) == (iota((width, width), 0) % run) * depth + iota((width, width), 0) // run
    ).astype(f32).astype(bf16)
    sketch_copy.wait()
    for g in range(depth):
        moved = dot(order, sketch[pl.ds(g * width, width), :]).astype(bf16)
        for l in range(depth):
            sorted_sketch[l, pl.ds(g * run, run), :] = moved[l * run : (l + 1) * run]

    flags = [
        [(charges_ref[0, l] == s - 1).astype(f32) for l in range(depth)] for s in range(3)
    ]
    for i in range(steps):
        slabs[i].wait()
        for g in range(MAP_ROWS // group):
            start = (i * MAP_ROWS + g * group) * phys
            grown = dot(spread, boundary[pl.ds(start, width), :])
            for l in range(depth):
                absorbed[l, pl.ds(g * group, group), :] = grown[l * group : (l + 1) * group]
        sums = [None] * 3
        for l in range(depth):
            high, low = split(absorbed[l])
            block = sorted_sketch[l]
            product = dot(high, block) + dot(low, block)
            for s in range(3):
                term = flags[s][l] * product
                sums[s] = term if sums[s] is None else sums[s] + term
        for s in range(3):
            high, low = split(sums[s])
            map_high[pl.ds(i * MAP_ROWS, MAP_ROWS), pl.ds(s * width, width)] = high
            map_low[pl.ds(i * MAP_ROWS, MAP_ROWS), pl.ds(s * width, width)] = low

    degree = (
        has_prev.astype(jnp.int32)
        + has_next.astype(jnp.int32)
        + has_below.astype(jnp.int32)
        + has_above.astype(jnp.int32)
    )
    pl.semaphore_wait(barrier, degree)

    def at(ref, k):
        return ref.at[pl.ds(k * CHUNK_ROWS, CHUNK_ROWS)]

    def state_copy(k):
        return pltpu.make_async_remote_copy(
            src_ref=at(out_ref, k), dst_ref=at(state, k), send_sem=state_send.at[k],
            recv_sem=state_recv.at[k], device_id=next_id, device_id_type=MESH,
        )

    def up_copy(k):
        return pltpu.make_async_remote_copy(
            src_ref=at(upward, k), dst_ref=at(from_below, k), send_sem=up_send.at[k],
            recv_sem=up_recv.at[k], device_id=above_id, device_id_type=MESH,
        )

    def down_copy(k):
        return pltpu.make_async_remote_copy(
            src_ref=at(downward, k), dst_ref=at(from_above, k), send_sem=down_send.at[k],
            recv_sem=down_recv.at[k], device_id=below_id, device_id_type=MESH,
        )

    def advance(k):
        @pl.when(has_prev)
        def _():
            state_copy(k).wait_recv()

        high, low = split(at(state, k)[...])

        def part(s):
            columns = pl.ds(s * width, width)
            return dot(high, map_high[:, columns]) + (
                dot(low, map_high[:, columns]) + dot(high, map_low[:, columns])
            )

        at(upward, k)[...] = part(2)

        @pl.when(has_above)
        def _():
            up_copy(k).start()

        at(downward, k)[...] = part(0)

        @pl.when(has_below)
        def _():
            down_copy(k).start()

        at(out_ref, k)[...] = part(1)

    def finish(k):
        @pl.when(has_below)
        def _():
            up_copy(k).wait_recv()
            at(out_ref, k)[...] += at(from_below, k)[...]

        @pl.when(has_above)
        def _():
            down_copy(k).wait_recv()
            at(out_ref, k)[...] += at(from_above, k)[...]

        @pl.when(has_next)
        def _():
            state_copy(k).start()

    for k in range(chunks + LAG):
        if k < chunks:
            advance(k)
        if k >= LAG:
            finish(k - LAG)

    for k in range(chunks):
        @pl.when(has_above)
        def _():
            up_copy(k).wait_send()

        @pl.when(has_below)
        def _():
            down_copy(k).wait_send()

        @pl.when(has_next)
        def _():
            state_copy(k).wait_send()


def local(sites, sectors, boundary, peps_row, sketch, charges, left_edge):
    _, width, phys, inner = boundary.shape
    depth = peps_row.shape[2]
    rows = left_edge.shape[0]
    chunks = rows // CHUNK_ROWS
    f32, bf16 = jnp.float32, jnp.bfloat16
    vmem = pl.BlockSpec(memory_space=pltpu.VMEM)
    hbm = pl.BlockSpec(memory_space=pl.ANY)
    dma = pltpu.SemaphoreType.DMA
    out = pl.pallas_call(
        functools.partial(kernel, sites, sectors, width, phys, depth),
        out_shape=jax.ShapeDtypeStruct((rows, width), f32),
        in_specs=[hbm, vmem, hbm, pl.BlockSpec(memory_space=pltpu.SMEM), vmem],
        out_specs=vmem,
        scratch_shapes=[
            pltpu.VMEM((width * phys, inner), bf16),
            pltpu.VMEM((width * depth, inner), bf16),
            pltpu.VMEM((depth, MAP_ROWS, inner), f32),
            pltpu.VMEM((depth, width, inner), bf16),
            pltpu.VMEM((width, 3 * inner), bf16),
            pltpu.VMEM((width, 3 * inner), bf16),
        ]
        + [pltpu.VMEM((rows, width), f32)] * 5
        + [dma((width // MAP_ROWS,)), dma(())]
        + [dma((chunks,))] * 6,
        compiler_params=pltpu.CompilerParams(collective_id=0, has_side_effects=True),
    )(
        boundary.reshape(width * phys, inner),
        peps_row[0].T,
        sketch.reshape(width * depth, inner),
        charges,
        left_edge,
    )
    return out[None]


def solution(mesh):
    in_specs = (
        P("site", "sector", None, None),
        P("site", None, None),
        P("site", "sector", None, None),
        P("site", None),
        P(None, "sector"),
    )
    out_specs = P("site", None, "sector")
    body = functools.partial(local, mesh.shape["site"], mesh.shape["sector"])
    return jax.shard_map(body, mesh=mesh, in_specs=in_specs, out_specs=out_specs, check_vma=False)
```

time: 127 us -> 45.7 us (0.36)
  the two profiles are of different devices: /device:TPU:8 before, /device:TPU:7 now
where the time goes in v1:
time: 45.7 us; the launch traced here: 45.5 us
  Pallas kernels  43.6 us (95%)
  local copies, waits for them, and re-layouts  1.87 us (4%)
    pallas_call x1, Pallas kernels, local(): pl.pallas_call(functools.partial(kernel, sites, sectors, width, phys, dep...  43.6 us
    unnamed x1, local copies, waits for them, and re-layouts  1.87 us

profile of v1, /device:TPU:7, one launch (start us, length us, event | category | flops | bytes accessed | tf_op | source)
XLA Modules:
  0.0 45.5 jit_solution(4859960925812418224)
XLA Ops:
  0.0 43.6 %shard_map.55 = f32[512,256]{1,0:T(8,128)} custom-call(bf16[8192,256]{1,0:T(8,128)(2,1)} %bitcast.6, bf16[8,32]{1,0:T(8,128)(2,1)} %bitcast.9, bf16[2048,256]{1,0:T(8,128)(2,1)} %bitcast.8, s32[1,8]{1,0:T(1,128)} %charges_ref.1, bf16[512,256]{1,0:T(8,128)(2,1)} %left_ref.1), custom_call_target="tpu_custom_call" | custom-call | tf_op jit(solution)/shard_map/pallas_call | solution.py:237
  43.6 1.9 %copy.7 = f32[1,512,256]{2,1,0:T(8,128)} copy(f32[1,512,256]{2,1,0:T(8,128)} %bitcast.7) | data formatting | bytes 1048576

commit v2 on v1

--- a/solution.py
+++ b/solution.py
@@ -9,8 +9,10 @@
 
 MESH = pl.DeviceIdType.MESH
 CHUNK_ROWS = 64
-LAG = 1
+LAG = 2
 MAP_ROWS = 64
+DOT_ROWS = 256
+SPLIT_MID = False
 
 
 def dot(a, b):
@@ -46,6 +48,7 @@
     from_above,
     upward,
     downward,
+    total,
     boundary_sem,
     sketch_sem,
     state_send,
@@ -54,6 +57,7 @@
     up_recv,
     down_send,
     down_recv,
+    result_sem,
 ):
     site = lax.axis_index("site")
     sector = lax.axis_index("sector")
@@ -92,6 +96,14 @@
     def _():
         state[...] = left_ref[...].astype(f32)
 
+    @pl.when(jnp.logical_not(has_below))
+    def _():
+        from_below[...] = jnp.zeros_like(from_below)
+
+    @pl.when(jnp.logical_not(has_above))
+    def _():
+        from_above[...] = jnp.zeros_like(from_above)
+
     group = width // phys
     size = group * depth
     iota = lambda shape, axis: lax.broadcasted_iota(jnp.int32, shape, axis)
@@ -116,23 +128,24 @@
     ]
     for i in range(steps):
         slabs[i].wait()
-        for g in range(MAP_ROWS // group):
-            start = (i * MAP_ROWS + g * group) * phys
-            grown = dot(spread, boundary[pl.ds(start, width), :])
+        for g in range(i * MAP_ROWS // group, (i + 1) * MAP_ROWS // group):
+            grown = dot(spread, boundary[pl.ds(g * group * phys, width), :])
             for l in range(depth):
                 absorbed[l, pl.ds(g * group, group), :] = grown[l * group : (l + 1) * group]
+    for i in range(width // DOT_ROWS):
+        part = pl.ds(i * DOT_ROWS, DOT_ROWS)
         sums = [None] * 3
         for l in range(depth):
-            high, low = split(absorbed[l])
-            block = sorted_sketch[l]
-            product = dot(high, block) + dot(low, block)
+            high, low = split(absorbed[l, part])
+            both = dot(jnp.concatenate([high, low], axis=0), sorted_sketch[l])
+            product = both[:DOT_ROWS] + both[DOT_ROWS:]
             for s in range(3):
                 term = flags[s][l] * product
                 sums[s] = term if sums[s] is None else sums[s] + term
         for s in range(3):
             high, low = split(sums[s])
-            map_high[pl.ds(i * MAP_ROWS, MAP_ROWS), pl.ds(s * width, width)] = high
-            map_low[pl.ds(i * MAP_ROWS, MAP_ROWS), pl.ds(s * width, width)] = low
+            map_high[part, pl.ds(s * width, width)] = high
+            map_low[part, pl.ds(s * width, width)] = low
 
     degree = (
         has_prev.astype(jnp.int32)
@@ -147,9 +160,12 @@
 
     def state_copy(k):
         return pltpu.make_async_remote_copy(
-            src_ref=at(out_ref, k), dst_ref=at(state, k), send_sem=state_send.at[k],
+            src_ref=at(total, k), dst_ref=at(state, k), send_sem=state_send.at[k],
             recv_sem=state_recv.at[k], device_id=next_id, device_id_type=MESH,
         )
+
+    def result_copy(k):
+        return pltpu.make_async_copy(at(total, k), at(out_ref, k), result_sem.at[k])
 
     def up_copy(k):
         return pltpu.make_async_remote_copy(
@@ -169,41 +185,45 @@
             state_copy(k).wait_recv()
 
         high, low = split(at(state, k)[...])
+        both = jnp.concatenate([high, low], axis=0)
 
         def part(s):
             columns = pl.ds(s * width, width)
-            return dot(high, map_high[:, columns]) + (
-                dot(low, map_high[:, columns]) + dot(high, map_low[:, columns])
-            )
+            twice = dot(both, map_high[:, columns])
+            return twice[:CHUNK_ROWS] + (twice[CHUNK_ROWS:] + dot(high, map_low[:, columns]))
 
         at(upward, k)[...] = part(2)
+        at(downward, k)[...] = part(0)
+        if not SPLIT_MID:
+            at(total, k)[...] = part(1)
 
         @pl.when(has_above)
         def _():
             up_copy(k).start()
 
-        at(downward, k)[...] = part(0)
-
         @pl.when(has_below)
         def _():
             down_copy(k).start()
 
-        at(out_ref, k)[...] = part(1)
+        if SPLIT_MID:
+            at(total, k)[...] = part(1)
 
     def finish(k):
         @pl.when(has_below)
         def _():
             up_copy(k).wait_recv()
-            at(out_ref, k)[...] += at(from_below, k)[...]
 
         @pl.when(has_above)
         def _():
             down_copy(k).wait_recv()
-            at(out_ref, k)[...] += at(from_above, k)[...]
+
+        at(total, k)[...] += at(from_below, k)[...] + at(from_above, k)[...]
 
         @pl.when(has_next)
         def _():
             state_copy(k).start()
+
+        result_copy(k).start()
 
     for k in range(chunks + LAG):
         if k < chunks:
@@ -212,6 +232,8 @@
             finish(k - LAG)
 
     for k in range(chunks):
+        result_copy(k).wait()
+
         @pl.when(has_above)
         def _():
             up_copy(k).wait_send()
@@ -238,18 +260,18 @@
         functools.partial(kernel, sites, sectors, width, phys, depth),
         out_shape=jax.ShapeDtypeStruct((rows, width), f32),
         in_specs=[hbm, vmem, hbm, pl.BlockSpec(memory_space=pltpu.SMEM), vmem],
-        out_specs=vmem,
+        out_specs=hbm,
         scratch_shapes=[
             pltpu.VMEM((width * phys, inner), bf16),
             pltpu.VMEM((width * depth, inner), bf16),
-            pltpu.VMEM((depth, MAP_ROWS, inner), f32),
+            pltpu.VMEM((depth, width, inner), f32),
             pltpu.VMEM((depth, width, inner), bf16),
             pltpu.VMEM((width, 3 * inner), bf16),
             pltpu.VMEM((width, 3 * inner), bf16),
         ]
-        + [pltpu.VMEM((rows, width), f32)] * 5
+        + [pltpu.VMEM((rows, width), f32)] * 6
         + [dma((width // MAP_ROWS,)), dma(())]
-        + [dma((chunks,))] * 6,
+        + [dma((chunks,))] * 7,
         compiler_params=pltpu.CompilerParams(collective_id=0, has_side_effects=True),
     )(
         boundary.reshape(width * phys, inner),

time: 45.7 us -> 41.8 us (0.915)
  Pallas kernels: 43.6 us -> 39.7 us
    pallas_call x1, Pallas kernels: 43.6 us -> 39.7 us  [local(): pl.pallas_call(functools.partial(kernel, sites, sectors, width, phys, dep...]
where the time goes in v2:
time: 41.8 us; the launch traced here: 41.6 us
  Pallas kernels  39.7 us (95%)
  local copies, waits for them, and re-layouts  1.87 us (4%)
    pallas_call x1, Pallas kernels, local(): pl.pallas_call(functools.partial(kernel, sites, sectors, width, phys, dep...  39.7 us
    unnamed x1, local copies, waits for them, and re-layouts  1.87 us

profile of v2, /device:TPU:7, one launch (start us, length us, event | category | flops | bytes accessed | tf_op | source)
XLA Modules:
  0.0 41.6 jit_solution(2264876336408234607)
XLA Ops:
  0.0 39.7 %shard_map.55 = f32[512,256]{1,0:T(8,128)} custom-call(bf16[8192,256]{1,0:T(8,128)(2,1)} %bitcast.6, bf16[8,32]{1,0:T(8,128)(2,1)} %bitcast.9, bf16[2048,256]{1,0:T(8,128)(2,1)} %bitcast.8, s32[1,8]{1,0:T(1,128)} %charges_ref.1, bf16[512,256]{1,0:T(8,128)(2,1)} %left_ref.1), custom_call_target="tpu_custom_call" | custom-call | tf_op jit(solution)/shard_map/pallas_call | solution.py:259
  39.8 1.9 %copy.7 = f32[1,512,256]{2,1,0:T(8,128)} copy(f32[1,512,256]{2,1,0:T(8,128)} %bitcast.7) | data formatting | bytes 1048576

commit v3 on v2

--- a/solution.py
+++ b/solution.py
@@ -8,8 +8,9 @@
 from jax.sharding import PartitionSpec as P
 
 MESH = pl.DeviceIdType.MESH
-CHUNK_ROWS = 64
-LAG = 2
+CHUNK_ROWS = 32
+LAG = 3
+LAG_FIRST = 4
 MAP_ROWS = 64
 DOT_ROWS = 256
 SPLIT_MID = False
@@ -225,11 +226,20 @@
 
         result_copy(k).start()
 
-    for k in range(chunks + LAG):
-        if k < chunks:
-            advance(k)
-        if k >= LAG:
-            finish(k - LAG)
+    def stream(lag):
+        for k in range(chunks + lag):
+            if k < chunks:
+                advance(k)
+            if k >= lag:
+                finish(k - lag)
+
+    @pl.when(site == 0)
+    def _():
+        stream(LAG_FIRST)
+
+    @pl.when(site > 0)
+    def _():
+        stream(LAG)
 
     for k in range(chunks):
         result_copy(k).wait()

time: 41.8 us -> 40.6 us (0.971)
  Pallas kernels: 39.7 us -> 38.3 us
    pallas_call x1, Pallas kernels: 39.7 us -> 38.3 us  [local(): pl.pallas_call(functools.partial(kernel, sites, sectors, width, phys, dep...]
where the time goes in v3:
time: 40.6 us; the launch traced here: 40.2 us
  Pallas kernels  38.3 us (94%)
  local copies, waits for them, and re-layouts  1.87 us (5%)
    pallas_call x1, Pallas kernels, local(): pl.pallas_call(functools.partial(kernel, sites, sectors, width, phys, dep...  38.3 us
    unnamed x1, local copies, waits for them, and re-layouts  1.87 us

profile of v3, /device:TPU:7, one launch (start us, length us, event | category | flops | bytes accessed | tf_op | source)
XLA Modules:
  0.0 40.2 jit_solution(8350369303158694238)
XLA Ops:
  0.0 38.3 %shard_map.55 = f32[512,256]{1,0:T(8,128)} custom-call(bf16[8192,256]{1,0:T(8,128)(2,1)} %bitcast.6, bf16[8,32]{1,0:T(8,128)(2,1)} %bitcast.9, bf16[2048,256]{1,0:T(8,128)(2,1)} %bitcast.8, s32[1,8]{1,0:T(1,128)} %charges_ref.1, bf16[512,256]{1,0:T(8,128)(2,1)} %left_ref.1), custom_call_target="tpu_custom_call" | custom-call | tf_op jit(solution)/shard_map/pallas_call | solution.py:269
  38.3 1.9 %copy.7 = f32[1,512,256]{2,1,0:T(8,128)} copy(f32[1,512,256]{2,1,0:T(8,128)} %bitcast.7) | data formatting | bytes 1048576

commit v4 on v3

--- a/solution.py
+++ b/solution.py
@@ -188,10 +188,11 @@
         high, low = split(at(state, k)[...])
         both = jnp.concatenate([high, low], axis=0)
 
+        twice = dot(both, map_high[...])
+        wide = twice[:CHUNK_ROWS] + (twice[CHUNK_ROWS:] + dot(high, map_low[...]))
+
         def part(s):
-            columns = pl.ds(s * width, width)
-            twice = dot(both, map_high[:, columns])
-            return twice[:CHUNK_ROWS] + (twice[CHUNK_ROWS:] + dot(high, map_low[:, columns]))
+            return wide[:, s * width : (s + 1) * width]
 
         at(upward, k)[...] = part(2)
         at(downward, k)[...] = part(0)

time: 40.6 us -> 40.7 us (level)
  no operation moved by 1% of the time
where the time goes in v4:
time: 40.7 us; the launch traced here: 40.2 us
  Pallas kernels  38.3 us (94%)
  local copies, waits for them, and re-layouts  1.87 us (5%)
    pallas_call x1, Pallas kernels, local(): pl.pallas_call(functools.partial(kernel, sites, sectors, width, phys, dep...  38.3 us
    unnamed x1, local copies, waits for them, and re-layouts  1.87 us

profile of v4, /device:TPU:7, one launch (start us, length us, event | category | flops | bytes accessed | tf_op | source)
XLA Modules:
  0.0 40.2 jit_solution(5466736064095675634)
XLA Ops:
  0.0 38.3 %shard_map.55 = f32[512,256]{1,0:T(8,128)} custom-call(bf16[8192,256]{1,0:T(8,128)(2,1)} %bitcast.6, bf16[8,32]{1,0:T(8,128)(2,1)} %bitcast.9, bf16[2048,256]{1,0:T(8,128)(2,1)} %bitcast.8, s32[1,8]{1,0:T(1,128)} %charges_ref.1, bf16[512,256]{1,0:T(8,128)(2,1)} %left_ref.1), custom_call_target="tpu_custom_call" | custom-call | tf_op jit(solution)/shard_map/pallas_call | solution.py:270
  38.3 1.9 %copy.7 = f32[1,512,256]{2,1,0:T(8,128)} copy(f32[1,512,256]{2,1,0:T(8,128)} %bitcast.7) | data formatting | bytes 1048576
